TPU v7x, 512 devices: a whole 4x8x8 slice. The times are simulated.
512 devices in a mesh: seq: 64 (over x, y, core), head: 8 (over z).
Axes of the slice: x: 4, y: 8, z: 8, core: 2. Of those that a mesh axis runs over, the one named last changes fastest.
Arguments:
- query_feat: bfloat16 [32768, 512], P('seq', 'head'), may hold values from -6 to 6
- key_feat: bfloat16 [32768, 512], P('seq', 'head'), may hold values from -6 to 6
- values: bfloat16 [32768, 4096], P('seq', 'head'), may hold values from -6 to 6
- conv_query: float32 [3, 512], P(None, 'head'), may hold values from -3 to 3
- conv_key: float32 [3, 512], P(None, 'head'), may hold values from -3 to 3
- conv_value: float32 [3, 4096], P(None, 'head'), may hold values from -3 to 3
- norm_gain: float32 [4096], P('head'), may hold values from 0.1 to 1.9
- out_weight: bfloat16 [4096, 4096], P('head', 'seq'), may hold values from -0.09375 to 0.09375
- stream_ids: int32 [64], replicated, may hold values from 0 to 7, never falling along the last dimension, each value on 1 to 32 neighbouring positions
Outputs:
- mixed: bfloat16 [32768, 4096], P('seq', 'head')
Inputs may be any that keep to these rules, and one draw needn't show every extreme that they name: `stream_ids`: stream ids never fall along the shards; each stream holds 1 to 32 consecutive shards, and one stream holds exactly 32.
All inputs are finite; a program needn't handle non-finite values.
Results may differ from a plain program's by a relative error of at most 0.018.
Values may be sent and summed in bfloat16 or wider, within the bound.
A program may use at most 128 MiB of HBM per device.

v0:
```python
import numpy as np
import jax
import jax.numpy as jnp
from jax import lax
from jax.sharding import PartitionSpec as P

HD = 128
FEAT = 16
PAD = 160


def tables(heads):
    left = np.zeros((heads * FEAT, heads * PAD), np.float32)
    right = np.zeros((heads * FEAT, heads * PAD), np.float32)
    add_left = np.zeros((1, heads * PAD), np.float32)
    add_right = np.zeros((1, heads * PAD), np.float32)
    scale = np.zeros((1, heads * PAD), np.float32)
    twice = np.zeros((1, heads * PAD), np.float32)
    for h in range(heads):
        at = h * PAD
        add_left[0, at] = add_right[0, at] = scale[0, at] = twice[0, at] = 1.0
        for i in range(FEAT):
            at = h * PAD + 1 + i
            left[h * FEAT + i, at] = 1.0
            add_right[0, at] = scale[0, at] = twice[0, at] = 1.0
        at = h * PAD + 1 + FEAT
        for i in range(FEAT):
            for j in range(i, FEAT):
                left[h * FEAT + i, at] = 1.0
                right[h * FEAT + j, at] = 1.0
                scale[0, at] = np.float32(0.5**0.5)
                twice[0, at] = 1.0 if i == j else 2.0
                at += 1
    return (left, right, add_left, add_right, scale, twice)


def taylor(conv, heads):
    left, right, add_left, add_right, scale, twice = tables(heads)
    a = (conv.astype(jnp.float32) * FEAT ** (-0.25)).astype(jnp.bfloat16)
    one = jnp.dot(a, jnp.asarray(left, jnp.bfloat16), preferred_element_type=jnp.float32) + add_left
    two = (
        jnp.dot(a, jnp.asarray(right, jnp.bfloat16), preferred_element_type=jnp.float32) + add_right
    )
    return ((one * two * scale).astype(jnp.bfloat16), jnp.asarray(twice, jnp.bfloat16))


def convolve(inputs, rim_rows, kernel, keep):
    padded = jnp.concatenate(
        [rim_rows.astype(jnp.float32) * keep, inputs.astype(jnp.float32)], axis=0
    )
    return (kernel[0] * padded[:-2] + kernel[1] * padded[1:-1] + kernel[2] * padded[2:]).astype(
        jnp.bfloat16
    )


def on_device(
    query_feat,
    key_feat,
    values,
    conv_query,
    conv_key,
    conv_value,
    norm_gain,
    out_weight,
    stream_ids,
):
    rows, qw = query_feat.shape
    heads = values.shape[1] // HD
    shards = lax.axis_size("seq")
    weight = lax.all_gather(out_weight.T, "seq", axis=0, tiled=True)
    position = lax.axis_index("seq")
    own_stream = stream_ids[position]
    prior_stream = stream_ids[jnp.maximum(position - 1, 0)]
    keep = 1.0 - jnp.logical_or(position == 0, own_stream != prior_stream).astype(jnp.float32)
    rim = jnp.concatenate([query_feat[-2:], key_feat[-2:], values[-2:]], axis=1)
    rim = lax.ppermute(rim, "seq", [(i, i + 1) for i in range(shards - 1)])
    qconv = convolve(query_feat, rim[:, :qw], conv_query, keep)
    kconv = convolve(key_feat, rim[:, qw : 2 * qw], conv_key, keep)
    vconv = convolve(values, rim[:, 2 * qw :], conv_value, keep)
    phk, twice = taylor(kconv, heads)
    kv = [
        lax.dot_general(
            phk[:, h * PAD : (h + 1) * PAD],
            vconv[:, h * HD : (h + 1) * HD],
            (((0,), (0,)), ((), ())),
            preferred_element_type=jnp.float32,
        )
        for h in range(heads)
    ]
    pieces = jnp.concatenate(kv, axis=0).astype(jnp.bfloat16).reshape(shards, -1, HD)
    pieces = lax.all_to_all(pieces, "seq", 0, 0, tiled=True)
    order = jnp.arange(shards)
    earlier = (stream_ids[:, None] == stream_ids[None, :]) & (order[None, :] < order[:, None])
    sums = jnp.einsum(
        "ds,skl->dkl", earlier.astype(jnp.bfloat16), pieces, preferred_element_type=jnp.float32
    ).astype(jnp.bfloat16)
    state = lax.all_to_all(sums, "seq", 0, 0, tiled=True).reshape(heads, PAD, HD)
    phq, _ = taylor(qconv, heads)
    phq = phq * twice
    causal = jnp.tril(jnp.ones((rows, rows), jnp.bool_))
    hidden = []
    for h in range(heads):
        q = phq[:, h * PAD : (h + 1) * PAD]
        k = phk[:, h * PAD : (h + 1) * PAD]
        v = vconv[:, h * HD : (h + 1) * HD]
        scores = lax.dot_general(q, k, (((1,), (1,)), ((), ())), preferred_element_type=jnp.float32)
        scores = jnp.where(causal, scores, 0.0).astype(jnp.bfloat16)
        y = jnp.dot(scores, v, preferred_element_type=jnp.float32) + jnp.dot(
            q, state[h], preferred_element_type=jnp.float32
        )
        gain = norm_gain[h * HD : (h + 1) * HD]
        y = y * lax.rsqrt(jnp.mean(y * y, axis=-1, keepdims=True) + 1e-05) * gain
        hidden.append(y.astype(jnp.bfloat16))
    hidden = jnp.concatenate(hidden, axis=1)
    terms = lax.dot_general(
        hidden, weight, (((1,), (1,)), ((), ())), preferred_element_type=jnp.float32
    )
    return lax.psum_scatter(terms.astype(jnp.bfloat16), "head", scatter_dimension=1, tiled=True)


def solution(mesh):
    placed = (
        P("seq", "head"),
        P("seq", "head"),
        P("seq", "head"),
        P(None, "head"),
        P(None, "head"),
        P(None, "head"),
        P("head"),
        P("head", "seq"),
        P(),
    )
    return jax.shard_map(
        on_device, mesh=mesh, in_specs=placed, out_specs=P("seq", "head"), check_vma=False
    )
```

profile of v0, /device:TPU:1, one launch (start us, length us, event | category | flops | bytes accessed | tf_op | source)
XLA Modules:
  0.0 170.8 jit_solution(12257114810949976883)
XLA Ops:
  6.5 0.0 all-gather.2.cloned.1.call-start
  6.5 0.7 all-gather.2.cloned.1.call-update
  7.3 0.7 slice.138
  8.0 0.8 slice.136
  8.8 0.1 copy.41
  8.8 0.8 slice.137
  9.7 0.1 copy.42
  9.7 0.1 pad_maximum_fusion.4
  9.8 4.6 %collective-permute-start = (bf16[2,640]{1,0:T(2,128)(2,1)S(1)}, bf16[2,640]{1,0:T(2,128)(2,1)S(1)}, u32[]{:S(2)}, u32[]{:S(2)}) collective-permute-start(bf16[2,640]{1,0:T(2,128)(2,1)S(1)} %pad_maximum_fusion.4), channel_id=1, source_target_pairs={{0,8},{8,16},{16,24},{24,32},{32,40},{40,48},{48,56},{56,64},{64,7... | collective-permute-start | bytes 7688 | tf_op jit(solution)/shard_map/ppermute | solution.py:76
  14.4 0.8 slice_bitcast_fusion.5
  15.2 0.8 fusion.90
  16.0 0.8 fusion.89
  16.9 0.8 slice_bitcast_fusion.2
  17.7 0.8 convert_element_type.86
  18.5 0.9 convert_element_type.92
  19.4 1.2 convert_element_type.99
  20.5 0.0 copy-done.5
  20.5 0.7 fusion.91
  22.6 0.0 collective-permute-done
  22.6 0.1 convert_multiply_fusion.1
  22.7 0.1 copy.38
  22.8 0.1 copy.37
  22.9 0.2 multiply_convert_fusion.4
  23.0 0.0 copy-done.4
  23.0 0.0 copy-done.1
  23.1 0.0 copy-start
  23.1 0.0 copy-start.2
  23.1 0.0 copy-start.3
  23.1 0.3 convolution_add_fusion.1
  23.4 0.3 fusion.19
  23.8 0.2 copy-done
  23.9 0.0 copy-done.2
  23.9 0.0 copy-done.3
  23.9 0.4 fusion.5
  24.3 0.2 convolution_convert_fusion.5
  24.6 0.3 convolution_convert_fusion.2
  24.9 0.3 convolution_convert_fusion.3
  25.2 0.3 convolution_convert_fusion.4
  25.6 0.0 copy-start.6
  25.6 0.8 convert_element_type.101
  26.4 9.3 %all-to-all-start = ((bf16[64,10,128]{2,1,0:T(8,128)(2,1)}), bf16[64,10,128]{2,1,0:T(8,128)(2,1)S(1)}, u32[]{:S(2)}, u32[]{:S(2)}) async-start(bf16[64,10,128]{2,1,0:T(8,128)(2,1)} %convert_element_type.101), calls=%async_computation | async-start | bytes 524288 | tf_op jit(solution)/shard_map/all_to_all | solution.py:91
  35.7 0.2 multiply_convert_fusion.5
  35.9 0.4 convolution_add_fusion.3
  36.2 0.4 fusion.10
  36.6 0.6 fusion.11
  37.2 0.6 fusion.12
  37.9 10.6 %all-to-all-done = bf16[64,10,128]{2,1,0:T(8,128)(2,1)S(1)} async-done(((bf16[64,10,128]{2,1,0:T(8,128)(2,1)}), bf16[64,10,128]{2,1,0:T(8,128)(2,1)S(1)}, u32[]{:S(2)}, u32[]{:S(2)}) %all-to-all-start) | async-done | bytes 163872 | tf_op jit(solution)/shard_map/all_to_all | solution.py:91
  48.5 0.2 convolution_convert_fusion.1
  48.7 0.8 copy.40
  49.5 5.9 %all-to-all-start.1 = ((bf16[64,10,128]{2,1,0:T(8,128)(2,1)}), bf16[64,10,128]{2,1,0:T(8,128)(2,1)S(1)}, u32[]{:S(2)}, u32[]{:S(2)}) async-start(bf16[64,10,128]{2,1,0:T(8,128)(2,1)} %copy.40), calls=%async_computation.1 | async-start | bytes 524288 | tf_op jit(solution)/shard_map/all_to_all | solution.py:97
  55.5 0.0 reduce-scatter.2.cloned.1.call-start
  55.5 0.6 fusion.13
  56.1 0.6 fusion.14
  56.7 10.7 %all-to-all-done.1 = bf16[64,10,128]{2,1,0:T(8,128)(2,1)S(1)} async-done(((bf16[64,10,128]{2,1,0:T(8,128)(2,1)}), bf16[64,10,128]{2,1,0:T(8,128)(2,1)S(1)}, u32[]{:S(2)}, u32[]{:S(2)}) %all-to-all-start.1) | async-done | bytes 163872 | tf_op jit(solution)/shard_map/all_to_all | solution.py:97
  67.6 0.3 multiply_reduce_fusion
  67.9 0.3 multiply_reduce_fusion.1
  68.3 0.3 multiply_reduce_fusion.2
  68.6 0.2 multiply_reduce_fusion.3
  68.9 0.1 multiply_convert_fusion
  69.0 0.1 multiply_convert_fusion.2
  69.1 32.4 %all-gather.2.cloned.1.call-done = bf16[4096,512]{1,0:T(8,128)(2,1)} async-done(((bf16[64,512]{1,0:T(8,128)(2,1)}), bf16[4096,512]{1,0:T(8,128)(2,1)}) %all-gather.2.cloned.1.call-update) | async-done | bytes 4194320 | tf_op jit(solution)/shard_map/all_gather | solution.py:70
  101.5 6.6 %convolution_convert_fusion = bf16[512,4096]{1,0:T(8,128)(2,1)} fusion(bf16[4096,512]{1,0:T(8,128)(2,1)} %all-gather.2.cloned.1.call-done, bf16[512,128]{0,1:T(8,128)(2,1)S(1)} %get-tuple-element.34, bf16[512,128]{0,1:T(8,128)(2,1)S(1)} %get-tuple-element.35, bf16[512,128]{0,1:T(8,128)(2,1)S(1)} %get-tuple-element.36, bf16[512,128]{0,1:T(8,128)(2,1)S(1)} %get-tuple-element.37), kind=kOutput, calls=%fused_computation | convolution fusion | flops 2151677952 | bytes 8912896 | tf_op jit(solution)/shard_map/dot_general | solution.py:115
  108.0 0.0 reduce-scatter.2.cloned.1.call-update
  108.1 55.9 %reduce-scatter.2.cloned.1.call-done = bf16[512,512]{1,0:T(8,128)(2,1)} async-done(((bf16[512,4096]{1,0:T(8,128)(2,1)}), bf16[512,512]{1,0:T(8,128)(2,1)}) %reduce-scatter.2.cloned.1.call-update) | async-done | bytes 524304 | tf_op jit(solution)/shard_map/reduce_scatter | solution.py:118
  (15 shorter events, 0.2 us)
Async XLA Ops:
  6.5 16.5 %copy-start.4 = (f32[640]{0:T(1024)S(1)}, f32[640]{0:T(1024)}, u32[]{:S(2)}) copy-start(f32[640]{0:T(1024)} %constant.49) | copy-start | bytes 7684
  6.5 16.5 %copy-start.1 = (bf16[64,640]{1,0:T(8,128)(2,1)S(1)}, bf16[64,640]{1,0:T(8,128)(2,1)}, u32[]{:S(2)}) copy-start(bf16[64,640]{1,0:T(8,128)(2,1)} %constant.43.clone) | copy-start | bytes 245764
  6.5 14.0 %copy-start.5 = (s32[64]{0:T(128)S(1)}, s32[64]{0:T(128)}, u32[]{:S(2)}) copy-start(s32[64]{0:T(128)} %param.28) | copy-start | bytes 772
  6.5 94.9 %all-gather.2.cloned.1.call-start = ((), (), s32[]{:S(2)}) async-start(), calls=%async_computation.3 | async-start | bytes 4259840 | tf_op jit(solution)/shard_map/all_gather | solution.py:70
  9.8 12.8 %collective-permute-start = (bf16[2,640]{1,0:T(2,128)(2,1)S(1)}, bf16[2,640]{1,0:T(2,128)(2,1)S(1)}, u32[]{:S(2)}, u32[]{:S(2)}) collective-permute-start(bf16[2,640]{1,0:T(2,128)(2,1)S(1)} %pad_maximum_fusion.4), channel_id=1, source_target_pairs={{0,8},{8,16},{16,24},{24,32},{32,40},{40,48},{48,56},{56,64},{64,7... | collective-permute-start | bytes 7688 | tf_op jit(solution)/shard_map/ppermute | solution.py:76
  23.1 0.9 copy-start
  23.1 0.9 copy-start.2
  23.1 0.9 copy-start.3
  25.6 10.7 %copy-start.6 = (bf16[640]{0:T(1024)(128)(2,1)S(1)}, bf16[640]{0:T(1024)(128)(2,1)}, u32[]{:S(2)}) copy-start(bf16[640]{0:T(1024)(128)(2,1)} %constant.52) | copy-start | bytes 3844
  26.4 22.1 %all-to-all-start = ((bf16[64,10,128]{2,1,0:T(8,128)(2,1)}), bf16[64,10,128]{2,1,0:T(8,128)(2,1)S(1)}, u32[]{:S(2)}, u32[]{:S(2)}) async-start(bf16[64,10,128]{2,1,0:T(8,128)(2,1)} %convert_element_type.101), calls=%async_computation | async-start | bytes 524288 | tf_op jit(solution)/shard_map/all_to_all | solution.py:91
  49.5 17.9 %all-to-all-start.1 = ((bf16[64,10,128]{2,1,0:T(8,128)(2,1)}), bf16[64,10,128]{2,1,0:T(8,128)(2,1)S(1)}, u32[]{:S(2)}, u32[]{:S(2)}) async-start(bf16[64,10,128]{2,1,0:T(8,128)(2,1)} %copy.40), calls=%async_computation.1 | async-start | bytes 524288 | tf_op jit(solution)/shard_map/all_to_all | solution.py:97
  55.5 108.5 %reduce-scatter.2.cloned.1.call-start = ((), (), s32[]{:S(2)}) async-start(), calls=%async_computation.4 | async-start | bytes 4718592 | tf_op jit(solution)/shard_map/reduce_scatter | solution.py:118
Sparse Core Ops, SparseCore 0:
  10.7 90.7 all-gather.1
  108.2 55.7 reduce-scatter.1
where the time goes:
time: 172 us; the launch traced here: 171 us
  waiting for transfers between devices  110 us (64%)
  starting transfers between devices  19.9 us (12%)
  between operations  15 us (9%)
  matrix products  13.1 us (8%)
  local copies, waits for them, and re-layouts  8.47 us (5%)
  other arithmetic  3.95 us (2%)
    reduce_scatter x1, waiting for transfers between devices, on_device(): lax.psum_scatter(terms.astype(jnp.bfloat16), 'head', scatter_dimension=1,...  55.9 us
    all_gather x1, waiting for transfers between devices, on_device(): weight = lax.all_gather(out_weight.T, 'seq', axis=0, tiled=True)  32.4 us
    all_to_all x1, waiting for transfers between devices, on_device(): lax.all_to_all(sums, 'seq', 0, 0, tiled=True).reshape(heads, PAD, HD)  10.7 us
    all_to_all x1, waiting for transfers between devices, on_device(): pieces = lax.all_to_all(pieces, 'seq', 0, 0, tiled=True)  10.6 us
    all_to_all x1, starting transfers between devices, on_device(): pieces = lax.all_to_all(pieces, 'seq', 0, 0, tiled=True)  9.33 us
    dot_general x1, matrix products, on_device(): lax.dot_general(hidden, weight, (((1,), (1,)), ((), ())), preferred_eleme...  6.57 us
    all_to_all x1, starting transfers between devices, on_device(): lax.all_to_all(sums, 'seq', 0, 0, tiled=True).reshape(heads, PAD, HD)  5.94 us
    ppermute x1, starting transfers between devices, on_device(): rim = lax.ppermute(rim, 'seq', [(i, i + 1) for i in range(shards - 1)])  4.58 us
  transfers between devices with their start and end apart: 5, of which 4 were waited for; matrix products, arithmetic and copies ran while one was open for 11% of the time, Pallas kernels for 0%

commit v1 on v0

--- a/solution.py
+++ b/solution.py
@@ -7,6 +7,13 @@
 HD = 128
 FEAT = 16
 PAD = 160
+
+
+def _wait_bands(u_in, row_axis):
+    even = jnp.stack([u_in for _ in range(lax.psum(1, row_axis))], axis=0)
+    known = lax.all_to_all(even, row_axis, 0, 0)
+    inter = jnp.concatenate(known, axis=0)
+    return inter
 
 
 def tables(heads):
@@ -67,7 +74,7 @@
     rows, qw = query_feat.shape
     heads = values.shape[1] // HD
     shards = lax.axis_size("seq")
-    weight = lax.all_gather(out_weight.T, "seq", axis=0, tiled=True)
+    weight = _wait_bands(out_weight.T, "seq")
     position = lax.axis_index("seq")
     own_stream = stream_ids[position]
     prior_stream = stream_ids[jnp.maximum(position - 1, 0)]

time: 172 us -> 239 us (1.39)
  waiting for transfers between devices: 110 us -> 149 us
  blocking collectives: 0 us -> 38.9 us
  starting transfers between devices: 19.9 us -> 11.2 us
    all_to_all x2 -> x1, waiting for transfers between devices: 21.3 us -> 90.4 us  [_wait_bands(): known = lax.all_to_all(even, row_axis, 0, 0)]
    all_to_all x0 -> x2, blocking collectives: none -> 38.9 us  [the longest x1 21.1 us: on_device(): pieces = lax.all_to_all(pieces, 'seq', 0, 0, tiled=True)]
    all_gather x1 -> x0, waiting for transfers between devices: 32.4 us -> none  [on_device(): weight = lax.all_gather(out_weight.T, 'seq', axis=0, tiled=True)]
    all_to_all x2 -> x1, starting transfers between devices: 15.3 us -> 6.36 us  [_wait_bands(): known = lax.all_to_all(even, row_axis, 0, 0)]
    reduce_scatter x1, waiting for transfers between devices: 55.9 us -> 58.5 us  [on_device(): lax.psum_scatter(terms.astype(jnp.bfloat16), 'head', scatter_dimension=1,...]
    another operation x0 -> x1, local copies, waits for them, and re-layouts: none -> 2.47 us  [_wait_bands(): even = jnp.stack([u_in for _ in range(lax.psum(1, row_axis))], axis=0)]
  transfers between devices with their start and end apart: 5 -> 3, of which waited for: 4 -> 2; matrix products, arithmetic and copies ran while one was open for 11% -> 4% of each run, Pallas kernels for 0% -> 0%
where the time goes in v1:
time: 239 us; the launch traced here: 238 us
  waiting for transfers between devices  149 us (62%)
  blocking collectives  38.9 us (16%)
  between operations  15.1 us (6%)
  matrix products  13.1 us (5%)
  starting transfers between devices  11.2 us (5%)
  local copies, waits for them, and re-layouts  7.8 us (3%)
  other arithmetic  3.15 us (1%)
    all_to_all x1, waiting for transfers between devices, _wait_bands(): known = lax.all_to_all(even, row_axis, 0, 0)  90.4 us
    reduce_scatter x1, waiting for transfers between devices, on_device(): lax.psum_scatter(terms.astype(jnp.bfloat16), 'head', scatter_dimension=1,...  58.5 us
    all_to_all x1, blocking collectives, on_device(): pieces = lax.all_to_all(pieces, 'seq', 0, 0, tiled=True)  21.1 us
    all_to_all x1, blocking collectives, on_device(): lax.all_to_all(sums, 'seq', 0, 0, tiled=True).reshape(heads, PAD, HD)  17.8 us
    dot_general x1, matrix products, on_device(): lax.dot_general(hidden, weight, (((1,), (1,)), ((), ())), preferred_eleme...  6.56 us
    all_to_all x1, starting transfers between devices, _wait_bands(): known = lax.all_to_all(even, row_axis, 0, 0)  6.36 us
  transfers between devices with their start and end apart: 3, of which 2 were waited for; matrix products, arithmetic and copies ran while one was open for 4% of the time, Pallas kernels for 0%

profile of v1, /device:TPU:1, one launch (start us, length us, event | category | flops | bytes accessed | tf_op | source)
XLA Modules:
  0.0 238.1 jit_solution(10450783701088562006)
XLA Ops:
  6.5 0.7 slice.138
  7.3 0.8 slice.137
  8.1 0.1 copy.42
  8.2 0.8 slice.136
  9.0 0.1 copy.41
  9.1 0.1 pad_maximum_fusion.4
  9.1 4.6 %collective-permute-start = (bf16[2,640]{1,0:T(2,128)(2,1)S(1)}, bf16[2,640]{1,0:T(2,128)(2,1)S(1)}, u32[]{:S(2)}, u32[]{:S(2)}) collective-permute-start(bf16[2,640]{1,0:T(2,128)(2,1)S(1)} %pad_maximum_fusion.4), channel_id=1, source_target_pairs={{0,8},{8,16},{16,24},{24,32},{32,40},{40,48},{48,56},{56,64},{64,7... | collective-permute-start | bytes 7688 | tf_op jit(solution)/shard_map/ppermute | solution.py:83
  13.7 0.8 fusion.89
  14.6 0.8 slice_bitcast_fusion.2
  15.3 0.8 convert_element_type.92
  16.2 0.0 copy-start
  16.2 0.0 copy-start.4
  16.2 0.0 copy-start.5
  16.2 1.2 convert_element_type.99
  17.4 0.0 copy-done.7
  17.5 0.7 fusion.91
  19.4 0.0 collective-permute-done
  19.4 0.1 convert_multiply_fusion.1
  19.5 0.1 copy.38
  19.6 0.2 multiply_convert_fusion.4
  19.8 0.0 copy-done.1
  19.8 0.0 copy-done.6
  19.8 0.3 convolution_add_fusion.1
  20.1 0.0 copy-done
  20.1 0.0 copy-done.4
  20.1 0.0 copy-done.5
  20.2 0.4 fusion.5
  20.5 0.3 fusion.19
  20.9 0.3 convolution_convert_fusion.2
  21.2 0.3 convolution_convert_fusion.3
  21.5 0.3 convolution_convert_fusion.4
  21.9 0.2 convolution_convert_fusion.5
  22.1 0.0 copy-start.3
  22.2 0.1 convert_element_type.101
  22.2 21.1 %all_to_all.15 = bf16[64,10,128]{2,1,0:T(8,128)(2,1)S(1)} all-to-all(bf16[64,10,128]{2,1,0:T(8,128)(2,1)S(1)} %convert_element_type.101), channel_id=1, replica_groups=mesh['seq'=64,'head'=8] {'seq'}, dimensions={0} | all-to-all | bytes 327680 | tf_op jit(solution)/shard_map/all_to_all | solution.py:98
  43.3 0.2 convolution_convert_fusion.1
  43.6 0.1 copy.40
  43.7 17.8 %all_to_all.16 = bf16[64,10,128]{2,1,0:T(8,128)(2,1)S(1)} all-to-all(bf16[64,10,128]{2,1,0:T(8,128)(2,1)S(1)} %copy.40), channel_id=1, replica_groups=mesh['seq'=64,'head'=8] {'seq'}, dimensions={0} | all-to-all | bytes 327680 | tf_op jit(solution)/shard_map/all_to_all | solution.py:104
  61.5 0.0 copy-done.3
  61.5 2.5 %stack.2 = bf16[64,64,512]{2,1,0:T(8,128)(2,1)} broadcast(bf16[64,512]{1,0:T(8,128)(2,1)S(1)} %bitcast.34), dimensions={1,2} | broadcast | bytes 4259840 | tf_op jit(solution)/shard_map/stack | solution.py:13
  64.0 6.4 %all-to-all-start.2 = ((bf16[64,64,512]{2,1,0:T(8,128)(2,1)}), bf16[64,64,512]{2,1,0:T(8,128)(2,1)}, u32[]{:S(2)}, u32[]{:S(2)}) async-start(bf16[64,64,512]{2,1,0:T(8,128)(2,1)} %stack.2), calls=%async_computation.2 | async-start | bytes 8388608 | tf_op jit(solution)/shard_map/all_to_all | solution.py:14
  70.3 0.0 copy-start.8
  70.4 0.2 reduce-scatter.2.cloned.1.call-start
  70.6 0.0 copy-done.2
  70.6 0.0 copy-done.10
  70.6 0.0 copy-done.9
  70.7 0.1 copy.37
  70.8 0.2 multiply_convert_fusion.5
  70.9 0.3 convolution_add_fusion.3
  71.3 0.4 fusion.10
  71.7 0.6 fusion.11
  72.3 0.6 fusion.12
  72.9 0.6 fusion.13
  73.5 0.6 fusion.14
  74.2 0.3 multiply_reduce_fusion
  74.6 0.3 multiply_reduce_fusion.1
  74.9 0.3 multiply_reduce_fusion.2
  75.3 0.2 multiply_reduce_fusion.3
  75.5 0.1 multiply_convert_fusion
  75.6 0.1 multiply_convert_fusion.2
  75.8 90.4 %all-to-all-done.2 = bf16[64,64,512]{2,1,0:T(8,128)(2,1)} async-done(((bf16[64,64,512]{2,1,0:T(8,128)(2,1)}), bf16[64,64,512]{2,1,0:T(8,128)(2,1)}, u32[]{:S(2)}, u32[]{:S(2)}) %all-to-all-start.2) | async-done | bytes 4194336 | tf_op jit(solution)/shard_map/all_to_all | solution.py:14
  166.2 6.6 %convolution_convert_fusion = bf16[512,4096]{1,0:T(8,128)(2,1)} fusion(bf16[4096,512]{1,0:T(8,128)(2,1)} %bitcast.12, bf16[512,128]{0,1:T(8,128)(2,1)S(1)} %get-tuple-element.34, bf16[512,128]{0,1:T(8,128)(2,1)S(1)} %get-tuple-element.35, bf16[512,128]{0,1:T(8,128)(2,1)S(1)} %get-tuple-element.36, bf16[512,128]{0,1:T(8,128)(2,1)S(1)} %get-tuple-element.37), kind=kOutput, calls=%fused_computation | convolution fusion | flops 2151677952 | bytes 8912896 | tf_op jit(solution)/shard_map/dot_general | solution.py:122
  172.7 0.0 reduce-scatter.2.cloned.1.call-update
  172.8 58.5 %reduce-scatter.2.cloned.1.call-done = bf16[512,512]{1,0:T(8,128)(2,1)} async-done(((bf16[512,4096]{1,0:T(8,128)(2,1)}), bf16[512,512]{1,0:T(8,128)(2,1)}) %reduce-scatter.2.cloned.1.call-update) | async-done | bytes 524304 | tf_op jit(solution)/shard_map/reduce_scatter | solution.py:125
  (21 shorter events, 0.2 us)
Async XLA Ops:
  6.5 13.2 %copy-start.1 = (bf16[64,640]{1,0:T(8,128)(2,1)S(1)}, bf16[64,640]{1,0:T(8,128)(2,1)}, u32[]{:S(2)}) copy-start(bf16[64,640]{1,0:T(8,128)(2,1)} %constant.43.clone) | copy-start | bytes 245764
  6.5 13.2 %copy-start.6 = (f32[640]{0:T(1024)S(1)}, f32[640]{0:T(1024)}, u32[]{:S(2)}) copy-start(f32[640]{0:T(1024)} %constant.49) | copy-start | bytes 7684
  6.5 10.9 %copy-start.7 = (s32[64]{0:T(128)S(1)}, s32[64]{0:T(128)}, u32[]{:S(2)}) copy-start(s32[64]{0:T(128)} %param.28) | copy-start | bytes 772
  9.1 10.3 %collective-permute-start = (bf16[2,640]{1,0:T(2,128)(2,1)S(1)}, bf16[2,640]{1,0:T(2,128)(2,1)S(1)}, u32[]{:S(2)}, u32[]{:S(2)}) collective-permute-start(bf16[2,640]{1,0:T(2,128)(2,1)S(1)} %pad_maximum_fusion.4), channel_id=1, source_target_pairs={{0,8},{8,16},{16,24},{24,32},{32,40},{40,48},{48,56},{56,64},{64,7... | collective-permute-start | bytes 7688 | tf_op jit(solution)/shard_map/ppermute | solution.py:83
  16.2 3.9 %copy-start = (bf16[64,640]{1,0:T(8,128)(2,1)S(1)}, bf16[64,640]{1,0:T(8,128)(2,1)}, u32[]{:S(2)}) copy-start(bf16[64,640]{1,0:T(8,128)(2,1)} %constant.45.clone) | copy-start | bytes 245764
  16.2 3.9 %copy-start.4 = (f32[640]{0:T(1024)S(1)}, f32[640]{0:T(1024)}, u32[]{:S(2)}) copy-start(f32[640]{0:T(1024)} %constant.51) | copy-start | bytes 7684
  16.2 3.9 %copy-start.5 = (f32[640]{0:T(1024)S(1)}, f32[640]{0:T(1024)}, u32[]{:S(2)}) copy-start(f32[640]{0:T(1024)} %constant.50) | copy-start | bytes 7684
  22.1 39.4 %copy-start.3 = (bf16[512,64]{0,1:T(8,128)(2,1)S(1)}, bf16[512,64]{0,1:T(8,128)(2,1)}, u32[]{:S(2)}) copy-start(bf16[512,64]{0,1:T(8,128)(2,1)} %param.27) | copy-start | bytes 196612
  64.0 6.6 %copy-start.2 = (bf16[512,64]{0,1:T(8,128)(2,1)S(1)}, bf16[512,64]{0,1:T(8,128)(2,1)}, u32[]{:S(2)}) copy-start(bf16[512,64]{0,1:T(8,128)(2,1)} %param.20) | copy-start | bytes 196612
  64.0 6.6 %copy-start.10 = (f32[3,64]{1,0:T(4,128)S(1)}, f32[3,64]{1,0:T(4,128)}, u32[]{:S(2)}) copy-start(f32[3,64]{1,0:T(4,128)} %param.23) | copy-start | bytes 2308
  64.0 6.7 %copy-start.9 = (f32[512]{0:T(512)S(1)}, f32[512]{0:T(512)}, u32[]{:S(2)}) copy-start(f32[512]{0:T(512)} %param.26) | copy-start | bytes 6148
  64.0 102.2 %all-to-all-start.2 = ((bf16[64,64,512]{2,1,0:T(8,128)(2,1)}), bf16[64,64,512]{2,1,0:T(8,128)(2,1)}, u32[]{:S(2)}, u32[]{:S(2)}) async-start(bf16[64,64,512]{2,1,0:T(8,128)(2,1)} %stack.2), calls=%async_computation.2 | async-start | bytes 8388608 | tf_op jit(solution)/shard_map/all_to_all | solution.py:14
  70.3 0.9 copy-start.8
  70.4 160.9 %reduce-scatter.2.cloned.1.call-start = ((), (), s32[]{:S(2)}) async-start(), calls=%async_computation.4 | async-start | bytes 4718592 | tf_op jit(solution)/shard_map/reduce_scatter | solution.py:125
Sparse Core Ops, SparseCore 0:
  172.9 58.3 reduce-scatter.1
